TPU v7x, 128 devices: a whole 4x4x4 slice. The times are simulated.
128 devices in a mesh: row: 16 (over y, x), col: 8 (over z, core).
Axes of the slice: x: 4, y: 4, z: 4, core: 2. Of those that a mesh axis runs over, the one named last changes fastest.
Arguments:
- row_emb: float32 [128, 300, 1024], P(('row', 'col')), may hold values from -1.5 to 1.5
- col_emb: float32 [128, 300, 1024], P(('row', 'col')), may hold values from -1.5 to 1.5
- row_acc: float32 [128, 300, 1024], P(('row', 'col')), may hold values from 0.5 to 8
- col_acc: float32 [128, 300, 1024], P(('row', 'col')), may hold values from 0.5 to 8
- marginal_log: float32 [131072], replicated, may hold values from -2 to 1
- tile_rows: int32 [384], P(('row', 'col')), may hold values from 0 to 127, as said below
- tile_cols: int32 [384], P(('row', 'col')), may hold values from 0 to 127, as said below
- counts: int32 [384, 1024, 1024], P(('row', 'col')), may hold values from 0 to 2047
Outputs:
- new_row_emb: float32 [128, 300, 1024], P(('row', 'col'))
- new_col_emb: float32 [128, 300, 1024], P(('row', 'col'))
- new_row_acc: float32 [128, 300, 1024], P(('row', 'col'))
- new_col_acc: float32 [128, 300, 1024], P(('row', 'col'))
Inputs may be any that keep to these rules, and one draw needn't show every extreme that they name: Block g of the embeddings lies on device g in the mesh's order (row slowest). Slot k lies on device p = k // 3; with p at row index r and col index c, tile_rows[k] // 8 equals r. With slot k on the device at col index c, tile_cols[k] % 8 equals c.
All inputs are finite; a program needn't handle non-finite values.
Results may differ from a plain program's by a relative error of at most 0.019.
Values may be sent and summed in bfloat16 or wider, within the bound.
No kernel may reach another device: no remote copies, remote signals or barrier semaphores. Data moves between devices by JAX's collectives and lax.ppermute only.
A program may use at most 128 MiB of HBM per device.

v0:
```python
import jax
import jax.numpy as jnp
from jax import lax
from jax.sharding import PartitionSpec as P

err_scale = 0.03125
learn_rate = 0.1


def split_up(array, dim, length):
    before, after = (array.shape[:dim], array.shape[dim + 1 :])
    return jnp.moveaxis(array.reshape(*before, length, -1, *after), dim, 0)


def sum_at_owner(array, axis, dim):
    length = lax.axis_size(axis)
    pieces = lax.all_to_all(split_up(array, dim, length), axis, 0, 0, tiled=True)
    return jnp.sum(pieces.astype(jnp.float32), axis=0)


def tile_terms(row_block, col_block, tile_counts, row_margin, col_margin):
    scores = lax.dot_general(
        row_block, col_block, (((0,), (0,)), ((), ())), preferred_element_type=jnp.float32
    )
    counted = tile_counts.astype(jnp.float32)
    shifted_log = jnp.log(jnp.maximum(counted, 1.0)) - row_margin[:, None] - col_margin[None, :]
    residue = scores - shifted_log
    weighted = (0.1 + 0.25 * jnp.sqrt(counted)) * residue
    cell_grad = jnp.where(tile_counts > 0, weighted, jax.nn.sigmoid(residue)) * err_scale
    errors = cell_grad.astype(jnp.bfloat16)
    row_term = lax.dot_general(
        col_block, errors, (((1,), (1,)), ((), ())), preferred_element_type=jnp.float32
    )
    col_term = jnp.dot(row_block, errors, preferred_element_type=jnp.float32)
    return (row_term, col_term)


def add_slot(buffer, slot_index, term):
    old_value = lax.dynamic_index_in_dim(buffer, slot_index, 0, keepdims=False)
    return lax.dynamic_update_index_in_dim(buffer, old_value + term, slot_index, 0)


def adagrad(weights, history, gradient):
    grown = history + gradient * gradient
    return (weights - learn_rate * gradient / jnp.sqrt(grown), grown)


def body(row_emb, col_emb, row_acc, col_acc, marginal_log, tile_rows, tile_cols, counts):
    col_count = lax.axis_size("col")
    row_count = lax.axis_size("row")
    emb_width = row_emb.shape[1]
    block_len = row_emb.shape[2]
    tile_total = counts.shape[0]
    row_low = row_emb.astype(jnp.bfloat16)
    col_low = col_emb.astype(jnp.bfloat16)
    rows_near = lax.all_gather(row_low, "col", axis=0, tiled=True)
    grads = (
        jnp.zeros((col_count, emb_width, block_len), jnp.float32),
        jnp.zeros((row_count, emb_width, block_len), jnp.float32),
    )
    cols_near = lax.all_gather(col_low, "row", axis=0, tiled=True)
    for tile_slot in range(tile_total):
        col_slot = tile_cols[tile_slot] // col_count
        col_block = lax.dynamic_index_in_dim(cols_near, col_slot, 0, keepdims=False)
        row_id = tile_rows[tile_slot]
        col_id = tile_cols[tile_slot]
        row_slot = row_id % col_count
        apply_col_slot = col_id // col_count
        row_block = lax.dynamic_index_in_dim(rows_near, row_slot, 0, keepdims=False)
        row_margin = lax.dynamic_slice_in_dim(marginal_log, row_id * block_len, block_len)
        col_margin = lax.dynamic_slice_in_dim(marginal_log, col_id * block_len, block_len)
        row_term, col_term = tile_terms(
            row_block, col_block, counts[tile_slot], row_margin, col_margin
        )
        grads = (
            add_slot(grads[0], row_slot, row_term),
            add_slot(grads[1], apply_col_slot, col_term),
        )
    row_sum = sum_at_owner(grads[0].astype(jnp.bfloat16), "col", 0)
    col_sum = lax.psum_scatter(
        grads[1].astype(jnp.bfloat16), "row", scatter_dimension=0, tiled=True
    ).astype(jnp.float32)
    new_row_emb, new_row_acc = adagrad(row_emb, row_acc, row_sum)
    new_col_emb, new_col_acc = adagrad(col_emb, col_acc, col_sum)
    return (new_row_emb, new_col_emb, new_row_acc, new_col_acc)


def solution(mesh):
    placed = (
        P(("row", "col"), None, None),
        P(("row", "col"), None, None),
        P(("row", "col"), None, None),
        P(("row", "col"), None, None),
        P(),
        P(("row", "col")),
        P(("row", "col")),
        P(("row", "col"), None, None),
    )
    return jax.shard_map(
        body,
        mesh=mesh,
        in_specs=placed,
        out_specs=(
            P(("row", "col"), None, None),
            P(("row", "col"), None, None),
            P(("row", "col"), None, None),
            P(("row", "col"), None, None),
        ),
        check_vma=False,
    )
```

profile of v0, /device:TPU:0, one launch (start us, length us, event | category | flops | bytes accessed | tf_op | source)
XLA Modules:
  0.0 274.2 jit_solution(9816080059861527763)
XLA Ops:
  7.2 2.3 copy.28
  9.6 2.3 copy.29
  12.0 0.6 fusion.64
  20.0 0.6 fusion.63
  30.0 0.8 fusion.62
  30.8 17.6 %all-gather.5.cloned.1.call-done = bf16[8,300,1024]{2,1,0:T(8,128)(2,1)} async-done(((bf16[1,300,1024]{2,1,0:T(8,128)(2,1)}), bf16[8,300,1024]{2,1,0:T(8,128)(2,1)}) %all-gather.5.cloned.1.call-update) | async-done | bytes 4915216 | tf_op jit(solution)/shard_map/all_gather | solution.py:56
  48.3 80.5 %all-gather.3.cloned.1.call-done = bf16[16,300,1024]{2,1,0:T(8,128)(2,1)} async-done(((bf16[1,300,1024]{2,1,0:T(8,128)(2,1)}), bf16[16,300,1024]{2,1,0:T(8,128)(2,1)}) %all-gather.3.cloned.1.call-update) | async-done | bytes 9830416 | tf_op jit(solution)/shard_map/all_gather | solution.py:61
  128.8 8.2 %fusion.14 = bf16[1024,1024]{1,0:T(8,128)(2,1)} fusion(s32[3,1024,1024]{2,1,0:T(8,128)} %param.15, f32[1024]{0:T(1024)S(1)} %get-tuple-element.17, f32[1024]{0:T(1024)S(1)} %get-tuple-element.18, bf16[8,300,1024]{2,1,0:T(8,128)(2,1)} %all-gather.5.cloned.1.call-done, s32[]{:T(128)S(6)} %select_n.95, ...), kind=kOutput, calls=%fused_computation.22 | convolution fusion | flops 644874240 | bytes 7544840 | tf_op jit(solution)/shard_map/dot_general | solution.py:22
  137.0 9.2 %broadcast_in_dim.36 = f32[16,300,1024]{2,1,0:T(8,128)} broadcast(f32[]{:T(128)} %constant.108.clone.1), dimensions={} | broadcast | bytes 19660804 | tf_op jit(solution)/shard_map/broadcast_in_dim | solution.py:59
  146.2 3.0 %fusion.23 = f32[16,300,1024]{2,1,0:T(8,128)} fusion(f32[16,300,1024]{2,1,0:T(8,128)} %broadcast_in_dim.36, s32[]{:T(128)S(6)} %select_n.93, bf16[1024,1024]{1,0:T(8,128)(2,1)S(1)} %copy-done.8, bf16[8,300,1024]{2,1,0:T(8,128)(2,1)} %all-gather.5.cloned.1.call-done, s32[]{:T(128)S(6)} %select_n.95), kind=kOutput, calls=%fused_computation.38 | convolution fusion | flops 629145600 | bytes 3964936 | tf_op jit(solution)/shard_map/dot_general | solution.py:34
  149.2 1.5 constant_dynamic-slice_fusion.3
  150.8 5.6 %fusion.9 = bf16[1024,1024]{1,0:T(8,128)(2,1)S(1)} fusion(s32[3,1024,1024]{2,1,0:T(8,128)S(1)} %bitcast.136, f32[1024]{0:T(1024)S(1)} %get-tuple-element.15, f32[1024]{0:T(1024)S(1)} %get-tuple-element.16, bf16[8,300,1024]{2,1,0:T(8,128)(2,1)} %all-gather.5.cloned.1.call-done, s32[]{:T(128)S(6)} %select_n.100, ...), kind=kOutput, calls=%fused_computation.15 | convolution fusion | flops 644874240 | bytes 7544840 | tf_op jit(solution)/shard_map/dot_general | solution.py:22
  156.4 0.5 slice-done.4
  156.9 1.9 fusion.18
  159.0 5.6 %fusion.4 = bf16[1024,1024]{1,0:T(8,128)(2,1)S(1)} fusion(s32[3,1024,1024]{2,1,0:T(8,128)S(1)} %bitcast.136, f32[1024]{0:T(1024)S(1)} %get-tuple-element.19, f32[1024]{0:T(1024)S(1)} %get-tuple-element.14, bf16[8,300,1024]{2,1,0:T(8,128)(2,1)} %all-gather.5.cloned.1.call-done, s32[]{:T(128)S(6)} %select_n.107, ...), kind=kOutput, calls=%fused_computation.8 | convolution fusion | flops 644874240 | bytes 7544840 | tf_op jit(solution)/shard_map/dot_general | solution.py:22
  164.6 1.3 copy-done.2
  165.9 1.9 fusion.16
  167.8 5.0 %convert_element_type.49 = bf16[16,300,1024]{2,1,0:T(8,128)(2,1)} convert(f32[16,300,1024]{2,1,0:T(8,128)S(1)} %fusion.16) | non-fusion elementwise | flops 4915200 | bytes 29491200 | tf_op jit(solution)/shard_map/convert_element_type | solution.py:81
  172.8 1.3 broadcast_in_dim.32
  174.4 1.9 fusion.24
  176.4 2.1 fusion.22
  178.6 1.9 fusion.20
  180.6 0.8 convert_bitcast_fusion
  181.4 62.3 %all_to_all.5 = bf16[8,1,300,1024]{3,2,1,0:T(8,128)(2,1)S(1)} all-to-all(bf16[8,1,300,1024]{3,2,1,0:T(8,128)(2,1)S(1)} %convert_bitcast_fusion), channel_id=1, replica_groups=mesh['row'=16,'col'=8] {'col'}, dimensions={0} | all-to-all | bytes 9830400 | tf_op jit(solution)/shard_map/all_to_all | solution.py:17
  243.7 1.1 convert_reduce_fusion
  244.9 0.4 multiply_bitcast_fusion
  245.2 0.5 copy-done.4
  245.8 5.8 %multiply_subtract_fusion = (f32[1,300,1024]{2,0,1:T(1,128)}, f32[1,300,1024]{2,0,1:T(1,128)}) fusion(f32[1,300,1024]{2,0,1:T(1,128)S(1)} %copy-done, f32[300,1024]{1,0:T(8,128)S(1)} %get-tuple-element.13, f32[1,300,1024]{2,0,1:T(1,128)S(1)} %copy-done.4, f32[1,300,1024]{2,1,0:T(8,128)S(1)} %get-tuple-element.12), kind=kLoop, calls=%fused_computation.47 | loop fusion | flops 921600 | bytes 7372800 | tf_op jit(solution)/shard_map/sub | solution.py:45
  251.6 9.8 %reduce-scatter.4.cloned.1.call-done = bf16[1,300,1024]{2,1,0:T(8,128)(2,1)} async-done(((bf16[16,300,1024]{2,1,0:T(8,128)(2,1)}), bf16[1,300,1024]{2,1,0:T(8,128)(2,1)}) %reduce-scatter.4.cloned.1.call-update) | async-done | bytes 614416
  261.4 1.8 fusion.26
  263.1 2.3 copy.21
  265.4 2.3 copy.22
  (44 shorter events, 0.9 us)
Async XLA Ops:
  7.2 4.8 %copy-start.6 = (s32[3]{0:T(128)S(1)}, s32[3]{0:T(128)}, u32[]{:S(2)}) copy-start(s32[3]{0:T(128)} %param.13) | copy-start | bytes 40
  7.2 12.9 %copy-start.7 = (s32[3]{0:T(128)S(1)}, s32[3]{0:T(128)}, u32[]{:S(2)}) copy-start(s32[3]{0:T(128)} %param.14) | copy-start | bytes 40
  7.2 41.2 %all-gather.5.cloned.1.call-start = ((), (), s32[]{:S(2)}) async-start(), calls=%async_computation.3 | async-start | bytes 5603328 | tf_op jit(solution)/shard_map/all_gather | solution.py:56
  9.6 119.3 %all-gather.3.cloned.1.call-start = ((), (), s32[]{:S(2)}) async-start(), calls=%async_computation.2 | async-start | bytes 10584064 | tf_op jit(solution)/shard_map/all_gather | solution.py:61
  11.9 249.4 %reduce-scatter.4.cloned.1.call-start = ((), (), s32[]{:S(2)}) async-start(), calls=%async_computation.4 | async-start | bytes 10584064
  128.8 21.9 %slice-start.5 = ((s8[12582912]{0:T(1024)(128)(4,1)}), s8[4194304]{0:T(1024)(128)(4,1)S(1)}, s32[]{:S(2)}) async-start(s8[12582912]{0:T(1024)(128)(4,1)} %bitcast.135), calls=%async_computation.10 | async-start | bytes 8388608
  128.8 21.9 %slice-start.6 = ((s8[12582912]{0:T(1024)(128)(4,1)}), s8[4194304]{0:T(1024)(128)(4,1)S(1)}, s32[]{:S(2)}) async-start(s8[12582912]{0:T(1024)(128)(4,1)} %bitcast.135), calls=%async_computation.11 | async-start | bytes 8388608
  137.0 9.3 %copy-start.8 = (bf16[1024,1024]{1,0:T(8,128)(2,1)S(1)}, bf16[1024,1024]{1,0:T(8,128)(2,1)}, u32[]{:S(2)}) copy-start(bf16[1024,1024]{1,0:T(8,128)(2,1)} %fusion.14) | copy-start | bytes 6291460
  137.0 13.8 %slice-start.7 = ((s8[12582912]{0:T(1024)(128)(4,1)}), s8[4194304]{0:T(1024)(128)(4,1)S(1)}, s32[]{:S(2)}) async-start(s8[12582912]{0:T(1024)(128)(4,1)} %bitcast.135), calls=%async_computation.12 | async-start | bytes 8388608
  149.2 7.2 %slice-start = ((s8[19922944]{0:T(1024)(128)(4,1)}), s8[4194304]{0:T(1024)(128)(4,1)S(1)}, s32[]{:S(2)}) async-start(s8[19922944]{0:T(1024)(128)(4,1)} %bitcast.133), calls=%async_computation.5 | async-start | bytes 8388608
  150.8 5.6 %slice-start.1 = ((s8[19922944]{0:T(1024)(128)(4,1)}), s8[4194304]{0:T(1024)(128)(4,1)S(1)}, s32[]{:S(2)}) async-start(s8[19922944]{0:T(1024)(128)(4,1)} %bitcast.133), calls=%async_computation.6 | async-start | bytes 8388608
  150.8 5.6 %slice-start.2 = ((s8[19922944]{0:T(1024)(128)(4,1)}), s8[4194304]{0:T(1024)(128)(4,1)S(1)}, s32[]{:S(2)}) async-start(s8[19922944]{0:T(1024)(128)(4,1)} %bitcast.133), calls=%async_computation.7 | async-start | bytes 8388608
  150.8 5.6 %slice-start.3 = ((s8[19922944]{0:T(1024)(128)(4,1)}), s8[4194304]{0:T(1024)(128)(4,1)S(1)}, s32[]{:S(2)}) async-start(s8[19922944]{0:T(1024)(128)(4,1)} %bitcast.133), calls=%async_computation.8 | async-start | bytes 8388608
  150.8 6.1 %slice-start.4 = ((s8[19922944]{0:T(1024)(128)(4,1)}), s8[3145728]{0:T(1024)(128)(4,1)S(1)}, s32[]{:S(2)}) async-start(s8[19922944]{0:T(1024)(128)(4,1)} %bitcast.133), calls=%async_computation.9 | async-start | bytes 6291456
  164.6 1.3 copy-start.2
  172.8 1.6 copy-start.9
  176.4 2.2 copy-start.3
  243.7 1.5 copy-start
  243.7 2.1 copy-start.4
  245.2 16.2 %copy-start.1 = (f32[1,300,1024]{2,0,1:T(1,128)S(1)}, f32[1,300,1024]{2,0,1:T(1,128)}, u32[]{:S(2)}) copy-start(f32[1,300,1024]{2,0,1:T(1,128)} %param.9) | copy-start | bytes 3686404
  245.2 16.1 %copy-start.5 = (f32[1,300,1024]{2,0,1:T(1,128)S(1)}, f32[1,300,1024]{2,0,1:T(1,128)}, u32[]{:S(2)}) copy-start(f32[1,300,1024]{2,0,1:T(1,128)} %param.11) | copy-start | bytes 3686404
Sparse Core Ops, SparseCore 0:
  10.3 38.0 all-gather.4
  51.0 77.7 all-gather.2
  172.9 88.4 reduce-scatter.3
where the time goes:
time: 275 us; the launch traced here: 274 us
  waiting for transfers between devices  108 us (39%)
  blocking collectives  62.3 us (23%)
  matrix products  32 us (12%)
  between operations  30.9 us (11%)
  local copies, waits for them, and re-layouts  26.2 us (10%)
  other arithmetic  14.8 us (5%)
    all_gather x1, waiting for transfers between devices, body(): cols_near = lax.all_gather(col_low, 'row', axis=0, tiled=True)  80.5 us
    all_to_all x1, blocking collectives, sum_at_owner(): lax.all_to_all(split_up(array, dim, length), axis, 0, 0, tiled=True)  62.3 us
    dot_general x3, matrix products, tile_terms(): lax.dot_general(row_block, col_block, (((0,), (0,)), ((), ())), preferred...  19.3 us
    all_gather x1, waiting for transfers between devices, body(): rows_near = lax.all_gather(row_low, 'col', axis=0, tiled=True)  17.6 us
    unnamed x40, local copies, waits for them, and re-layouts  11.9 us
    unnamed x4, waiting for transfers between devices  9.82 us
    broadcast_in_dim x1, local copies, waits for them, and re-layouts, body(): jnp.zeros((row_count, emb_width, block_len), jnp.float32)  9.25 us
    sub x2, other arithmetic, adagrad(): return (weights - learn_rate * gradient / jnp.sqrt(grown), grown)  7.58 us
  transfers between devices with their start and end apart: 3, of which 3 were waited for; matrix products, arithmetic and copies ran while one was open for 7% of the time, Pallas kernels for 0%

commit v1 on v0

--- a/solution.py
+++ b/solution.py
@@ -2,6 +2,7 @@
 import jax.numpy as jnp
 from jax import lax
 from jax.sharding import PartitionSpec as P
+from jax.lax import all_to_all, axis_size
 
 err_scale = 0.03125
 learn_rate = 0.1
@@ -53,7 +54,9 @@
     tile_total = counts.shape[0]
     row_low = row_emb.astype(jnp.bfloat16)
     col_low = col_emb.astype(jnp.bfloat16)
-    rows_near = lax.all_gather(row_low, "col", axis=0, tiled=True)
+    devs = axis_size("col")
+    tray = tuple((devs if no == 0 else 1 for no in range(row_low.ndim)))
+    rows_near = all_to_all(jnp.tile(row_low, tray), "col", split_axis=0, concat_axis=0, tiled=True)
     grads = (
         jnp.zeros((col_count, emb_width, block_len), jnp.float32),
         jnp.zeros((row_count, emb_width, block_len), jnp.float32),

time: 275 us -> 238 us (0.87)
  waiting for transfers between devices: 108 us -> 61.2 us
  starting transfers between devices: 0.12 us -> 5.63 us
    all_gather x1, waiting for transfers between devices: 80.5 us -> 12.6 us  [body(): cols_near = lax.all_gather(col_low, 'row', axis=0, tiled=True)]
    all_to_all x0 -> x1, waiting for transfers between devices: none -> 38.5 us  [body(): all_to_all(jnp.tile(row_low, tray), 'col', split_axis=0, concat_axis=0, t...]
    all_gather x1 -> x0, waiting for transfers between devices: 17.6 us -> none  [body(): rows_near = lax.all_gather(row_low, 'col', axis=0, tiled=True)]
    all_to_all x0 -> x1, starting transfers between devices: none -> 5.56 us  [body(): all_to_all(jnp.tile(row_low, tray), 'col', split_axis=0, concat_axis=0, t...]
    another operation x0 -> x1, local copies, waits for them, and re-layouts: none -> 2.89 us  [body(): jnp.tile(row_low, tray)]
    unnamed x4 -> x3, waiting for transfers between devices: 9.82 us -> 10.2 us
  transfers between devices with their start and end apart: 3 -> 3, of which waited for: 3 -> 3; matrix products, arithmetic and copies ran while one was open for 7% -> 10% of each run, Pallas kernels for 0% -> 0%
where the time goes in v1:
time: 238 us; the launch traced here: 237 us
  blocking collectives  62.3 us (26%)
  waiting for transfers between devices  61.2 us (26%)
  matrix products  32 us (13%)
  between operations  32 us (13%)
  local copies, waits for them, and re-layouts  26.8 us (11%)
  other arithmetic  17 us (7%)
  starting transfers between devices  5.63 us (2%)
    all_to_all x1, blocking collectives, sum_at_owner(): lax.all_to_all(split_up(array, dim, length), axis, 0, 0, tiled=True)  62.3 us
    all_to_all x1, waiting for transfers between devices, body(): all_to_all(jnp.tile(row_low, tray), 'col', split_axis=0, concat_axis=0, t...  38.5 us
    dot_general x3, matrix products, tile_terms(): lax.dot_general(row_block, col_block, (((0,), (0,)), ((), ())), preferred...  19.3 us
    all_gather x1, waiting for transfers between devices, body(): cols_near = lax.all_gather(col_low, 'row', axis=0, tiled=True)  12.6 us
    unnamed x3, waiting for transfers between devices  10.2 us
    unnamed x40, local copies, waits for them, and re-layouts  9.65 us
    broadcast_in_dim x1, local copies, waits for them, and re-layouts, body(): jnp.zeros((row_count, emb_width, block_len), jnp.float32)  9.25 us
    sub x2, other arithmetic, adagrad(): return (weights - learn_rate * gradient / jnp.sqrt(grown), grown)  7.58 us
  transfers between devices with their start and end apart: 3, of which 3 were waited for; matrix products, arithmetic and copies ran while one was open for 10% of the time, Pallas kernels for 0%

profile of v1, /device:TPU:0, one launch (start us, length us, event | category | flops | bytes accessed | tf_op | source)
XLA Modules:
  0.0 237.1 jit_solution(12771290345418457833)
XLA Ops:
  7.2 2.3 copy.28
  9.5 2.1 convert_element_type.41
  11.9 2.9 %tile.10 = bf16[8,300,1024]{2,1,0:T(8,128)(2,1)} broadcast(bf16[300,1024]{1,0:T(8,128)(2,1)S(1)} %bitcast.138), dimensions={1,2} | broadcast | bytes 5529600 | tf_op jit(solution)/shard_map/tile | solution.py:59
  14.8 5.6 %all-to-all-start = ((bf16[8,300,1024]{2,1,0:T(8,128)(2,1)}), bf16[8,300,1024]{2,1,0:T(8,128)(2,1)}, u32[]{:S(2)}, u32[]{:S(2)}) async-start(bf16[8,300,1024]{2,1,0:T(8,128)(2,1)} %tile.10), calls=%async_computation | async-start | bytes 9961472 | tf_op jit(solution)/shard_map/all_to_all | solution.py:59
  20.4 0.6 fusion.64
  28.8 0.6 fusion.63
  39.2 0.8 fusion.62
  40.0 38.5 %all-to-all-done = bf16[8,300,1024]{2,1,0:T(8,128)(2,1)} async-done(((bf16[8,300,1024]{2,1,0:T(8,128)(2,1)}), bf16[8,300,1024]{2,1,0:T(8,128)(2,1)}, u32[]{:S(2)}, u32[]{:S(2)}) %all-to-all-start) | async-done | bytes 4915232 | tf_op jit(solution)/shard_map/all_to_all | solution.py:59
  78.5 12.6 %all-gather.2.cloned.1.call-done = bf16[16,300,1024]{2,1,0:T(8,128)(2,1)} async-done(((bf16[1,300,1024]{2,1,0:T(8,128)(2,1)}), bf16[16,300,1024]{2,1,0:T(8,128)(2,1)}) %all-gather.2.cloned.1.call-update) | async-done | bytes 9830416 | tf_op jit(solution)/shard_map/all_gather | solution.py:64
  91.1 8.2 %fusion.14 = bf16[1024,1024]{1,0:T(8,128)(2,1)} fusion(s32[3,1024,1024]{2,1,0:T(8,128)} %param.15, f32[1024]{0:T(1024)S(1)} %get-tuple-element.17, f32[1024]{0:T(1024)S(1)} %get-tuple-element.18, bf16[8,300,1024]{2,1,0:T(8,128)(2,1)} %all-to-all-done, s32[]{:T(128)S(6)} %select_n.95, bf16[16,300,1024]{2,1,0:T(8,128)(2,1)} %all-gather.2.cloned.1.call-done, ...), kind=kOutput, calls=%fused_computation.22 | convolution fusion | flops 644874240 | bytes 7544840 | tf_op jit(solution)/shard_map/dot_general | solution.py:23
  99.2 9.3 %broadcast_in_dim.36 = f32[16,300,1024]{2,1,0:T(8,128)} broadcast(f32[]{:T(128)} %constant.108.clone.1), dimensions={} | broadcast | bytes 19660804 | tf_op jit(solution)/shard_map/broadcast_in_dim | solution.py:62
  108.5 3.0 %fusion.23 = f32[16,300,1024]{2,1,0:T(8,128)} fusion(f32[16,300,1024]{2,1,0:T(8,128)} %broadcast_in_dim.36, s32[]{:T(128)S(6)} %select_n.93, bf16[1024,1024]{1,0:T(8,128)(2,1)S(1)} %copy-done.8, bf16[8,300,1024]{2,1,0:T(8,128)(2,1)} %all-to-all-done, s32[]{:T(128)S(6)} %select_n.95), kind=kOutput, calls=%fused_computation.38 | convolution fusion | flops 629145600 | bytes 3964936 | tf_op jit(solution)/shard_map/dot_general | solution.py:35
  111.5 1.5 constant_dynamic-slice_fusion.3
  113.1 5.6 %fusion.9 = bf16[1024,1024]{1,0:T(8,128)(2,1)S(1)} fusion(s32[3,1024,1024]{2,1,0:T(8,128)S(1)} %bitcast.140, f32[1024]{0:T(1024)S(1)} %get-tuple-element.15, f32[1024]{0:T(1024)S(1)} %get-tuple-element.16, bf16[8,300,1024]{2,1,0:T(8,128)(2,1)} %all-to-all-done, s32[]{:T(128)S(6)} %select_n.100, bf16[16,300,1024]{2,1,0:T(8,128)(2,1)} %all-gather.2.cloned.1.call-done, ...), kind=kOutput, calls=%fused_computation.15 | convolution fusion | flops 644874240 | bytes 7544840 | tf_op jit(solution)/shard_map/dot_general | solution.py:23
  118.7 0.5 slice-done.4
  119.2 1.9 fusion.18
  121.2 5.6 %fusion.4 = bf16[1024,1024]{1,0:T(8,128)(2,1)S(1)} fusion(s32[3,1024,1024]{2,1,0:T(8,128)S(1)} %bitcast.140, f32[1024]{0:T(1024)S(1)} %get-tuple-element.19, f32[1024]{0:T(1024)S(1)} %get-tuple-element.14, bf16[8,300,1024]{2,1,0:T(8,128)(2,1)} %all-to-all-done, s32[]{:T(128)S(6)} %select_n.107, bf16[16,300,1024]{2,1,0:T(8,128)(2,1)} %all-gather.2.cloned.1.call-done, ...), kind=kOutput, calls=%fused_computation.8 | convolution fusion | flops 644874240 | bytes 7544840 | tf_op jit(solution)/shard_map/dot_general | solution.py:23
  126.8 1.3 copy-done.2
  128.1 1.9 fusion.16
  130.0 5.0 %convert_element_type.49 = bf16[16,300,1024]{2,1,0:T(8,128)(2,1)} convert(f32[16,300,1024]{2,1,0:T(8,128)S(1)} %fusion.16) | non-fusion elementwise | flops 4915200 | bytes 29491200 | tf_op jit(solution)/shard_map/convert_element_type | solution.py:84
  135.1 1.3 broadcast_in_dim.32
  136.7 1.9 fusion.24
  138.7 2.1 fusion.22
  140.9 1.9 fusion.20
  142.9 0.8 convert_bitcast_fusion
  143.6 62.3 %all_to_all.10 = bf16[8,1,300,1024]{3,2,1,0:T(8,128)(2,1)S(1)} all-to-all(bf16[8,1,300,1024]{3,2,1,0:T(8,128)(2,1)S(1)} %convert_bitcast_fusion), channel_id=1, replica_groups=mesh['row'=16,'col'=8] {'col'}, dimensions={0} | all-to-all | bytes 9830400 | tf_op jit(solution)/shard_map/all_to_all | solution.py:18
  206.0 1.1 convert_reduce_fusion
  207.9 5.8 %multiply_subtract_fusion = (f32[1,300,1024]{2,0,1:T(1,128)}, f32[1,300,1024]{2,0,1:T(1,128)}) fusion(f32[1,300,1024]{2,0,1:T(1,128)S(1)} %copy-done, f32[300,1024]{1,0:T(8,128)S(1)} %get-tuple-element.13, f32[1,300,1024]{2,0,1:T(1,128)S(1)} %copy-done.4, f32[1,300,1024]{2,1,0:T(8,128)S(1)} %get-tuple-element.12), kind=kLoop, calls=%fused_computation.46 | loop fusion | flops 921600 | bytes 7372800 | tf_op jit(solution)/shard_map/sub | solution.py:46
  213.7 10.1 %reduce-scatter.4.cloned.1.call-done = bf16[1,300,1024]{2,1,0:T(8,128)(2,1)} async-done(((bf16[16,300,1024]{2,1,0:T(8,128)(2,1)}), bf16[1,300,1024]{2,1,0:T(8,128)(2,1)}) %reduce-scatter.4.cloned.1.call-update) | async-done | bytes 614416
  223.9 1.8 fusion.26
  225.6 2.3 copy.20
  227.9 2.3 copy.21
  (45 shorter events, 1.8 us)
Async XLA Ops:
  7.2 83.9 %all-gather.2.cloned.1.call-start = ((), (), s32[]{:S(2)}) async-start(), calls=%async_computation.3 | async-start | bytes 10584064 | tf_op jit(solution)/shard_map/all_gather | solution.py:64
  14.8 5.6 %copy-start.6 = (s32[3]{0:T(128)S(1)}, s32[3]{0:T(128)}, u32[]{:S(2)}) copy-start(s32[3]{0:T(128)} %param.13) | copy-start | bytes 40
  14.8 14.0 %copy-start.7 = (s32[3]{0:T(128)S(1)}, s32[3]{0:T(128)}, u32[]{:S(2)}) copy-start(s32[3]{0:T(128)} %param.14) | copy-start | bytes 40
  14.8 63.7 %all-to-all-start = ((bf16[8,300,1024]{2,1,0:T(8,128)(2,1)}), bf16[8,300,1024]{2,1,0:T(8,128)(2,1)}, u32[]{:S(2)}, u32[]{:S(2)}) async-start(bf16[8,300,1024]{2,1,0:T(8,128)(2,1)} %tile.10), calls=%async_computation | async-start | bytes 9961472 | tf_op jit(solution)/shard_map/all_to_all | solution.py:59
  20.3 203.5 %reduce-scatter.4.cloned.1.call-start = ((), (), s32[]{:S(2)}) async-start(), calls=%async_computation.4 | async-start | bytes 10584064
  91.1 21.9 %slice-start.5 = ((s8[12582912]{0:T(1024)(128)(4,1)}), s8[4194304]{0:T(1024)(128)(4,1)S(1)}, s32[]{:S(2)}) async-start(s8[12582912]{0:T(1024)(128)(4,1)} %bitcast.139), calls=%async_computation.10 | async-start | bytes 8388608
  91.1 21.9 %slice-start.6 = ((s8[12582912]{0:T(1024)(128)(4,1)}), s8[4194304]{0:T(1024)(128)(4,1)S(1)}, s32[]{:S(2)}) async-start(s8[12582912]{0:T(1024)(128)(4,1)} %bitcast.139), calls=%async_computation.11 | async-start | bytes 8388608
  99.2 9.3 %copy-start.8 = (bf16[1024,1024]{1,0:T(8,128)(2,1)S(1)}, bf16[1024,1024]{1,0:T(8,128)(2,1)}, u32[]{:S(2)}) copy-start(bf16[1024,1024]{1,0:T(8,128)(2,1)} %fusion.14) | copy-start | bytes 6291460
  99.2 13.8 %slice-start.7 = ((s8[12582912]{0:T(1024)(128)(4,1)}), s8[4194304]{0:T(1024)(128)(4,1)S(1)}, s32[]{:S(2)}) async-start(s8[12582912]{0:T(1024)(128)(4,1)} %bitcast.139), calls=%async_computation.12 | async-start | bytes 8388608
  111.5 7.2 %slice-start = ((s8[19922944]{0:T(1024)(128)(4,1)}), s8[4194304]{0:T(1024)(128)(4,1)S(1)}, s32[]{:S(2)}) async-start(s8[19922944]{0:T(1024)(128)(4,1)} %bitcast.136), calls=%async_computation.5 | async-start | bytes 8388608
  113.0 5.6 %slice-start.1 = ((s8[19922944]{0:T(1024)(128)(4,1)}), s8[4194304]{0:T(1024)(128)(4,1)S(1)}, s32[]{:S(2)}) async-start(s8[19922944]{0:T(1024)(128)(4,1)} %bitcast.136), calls=%async_computation.6 | async-start | bytes 8388608
  113.0 5.6 %slice-start.2 = ((s8[19922944]{0:T(1024)(128)(4,1)}), s8[4194304]{0:T(1024)(128)(4,1)S(1)}, s32[]{:S(2)}) async-start(s8[19922944]{0:T(1024)(128)(4,1)} %bitcast.136), calls=%async_computation.7 | async-start | bytes 8388608
  113.0 5.6 %slice-start.3 = ((s8[19922944]{0:T(1024)(128)(4,1)}), s8[4194304]{0:T(1024)(128)(4,1)S(1)}, s32[]{:S(2)}) async-start(s8[19922944]{0:T(1024)(128)(4,1)} %bitcast.136), calls=%async_computation.8 | async-start | bytes 8388608
  113.1 6.1 %slice-start.4 = ((s8[19922944]{0:T(1024)(128)(4,1)}), s8[3145728]{0:T(1024)(128)(4,1)S(1)}, s32[]{:S(2)}) async-start(s8[19922944]{0:T(1024)(128)(4,1)} %bitcast.136), calls=%async_computation.9 | async-start | bytes 6291456
  126.8 1.3 copy-start.2
  135.1 1.6 copy-start.9
  138.7 2.2 copy-start.3
  206.0 1.5 copy-start
  206.0 1.9 copy-start.4
  207.5 16.4 %copy-start.1 = (f32[1,300,1024]{2,0,1:T(1,128)S(1)}, f32[1,300,1024]{2,0,1:T(1,128)}, u32[]{:S(2)}) copy-start(f32[1,300,1024]{2,0,1:T(1,128)} %param.9) | copy-start | bytes 3686404
  207.5 16.4 %copy-start.5 = (f32[1,300,1024]{2,0,1:T(1,128)S(1)}, f32[1,300,1024]{2,0,1:T(1,128)}, u32[]{:S(2)}) copy-start(f32[1,300,1024]{2,0,1:T(1,128)} %param.11) | copy-start | bytes 3686404
Sparse Core Ops, SparseCore 0:
  10.7 80.3 all-gather.1
  135.2 88.6 reduce-scatter.3
